TPU v7x, 32 devices: a whole 2x2x4 slice. The times are simulated.
32 devices in a mesh: ctx: 8 (over z, x), head: 4 (over y, core).
Axes of the slice: x: 2, y: 2, z: 4, core: 2. Of those that a mesh axis runs over, the one named last changes fastest.
Arguments:
- video_rows: bfloat16 [4096, 5120], P('ctx'), may hold values from -6 to 6
- w_query: bfloat16 [5120, 5120], P('ctx', 'head'), may hold values from -0.078125 to 0.078125
- w_output: bfloat16 [5120, 5120], P('ctx', 'head'), may hold values from -0.078125 to 0.078125
- audio_tokens: bfloat16 [2, 32, 768], P(None, 'ctx'), may hold values from -544 to 544
- w_key: bfloat16 [768, 5120], P(None, 'head'), may hold values from -0.21875 to 0.21875
- w_value: bfloat16 [768, 5120], P(None, 'head'), may hold values from -0.21875 to 0.21875
- row_lists: int32 [2, 4096], P(None, 'ctx'), may hold values from 0 to 511, as said below
- row_counts: int32 [2, 8], P(None, 'ctx'), may hold values from 0 to 512, as said below
Outputs:
- layer_out: bfloat16 [4096, 5120], P('ctx', 'head')
Inputs may be any that keep to these rules, and one draw needn't show every extreme that they name: `row_lists`: the first row_counts[s, c] entries of speaker s's block on shard c are distinct, live entries of the two speakers on one shard are distinct rows, and the other entries are arbitrary row numbers of the shard. `row_counts`: on each shard the two counts add up to at most 512.
All inputs are finite; a program needn't handle non-finite values.
Results may differ from a plain program's by a relative error of at most 0.0045.
The roundings to bfloat16 on the way count: a program that leaves them out, or rounds other values in their place, can miss the bound.
Values may be sent and summed in bfloat16 or wider, within the bound.
No kernel may reach another device: no remote copies, remote signals or barrier semaphores. Data moves between devices by JAX's collectives and lax.ppermute only.
A program may use at most 128 MiB of HBM per device.

v0:
```python
import jax
import jax.numpy as jnp
from jax import lax
from jax.sharding import PartitionSpec as P

HD = 128
SPK = 2


def add_rows(left_rows, shard_piece):
    return jnp.dot(left_rows, shard_piece, preferred_element_type=jnp.float32)


def shards(video_rows, w_query, w_output, audio_tokens, w_key, w_value, row_lists, row_counts):
    rows_dev = video_rows.shape[0]
    columns = w_query.shape[1]
    heads_dev = columns // HD
    queries = add_rows(video_rows, lax.all_gather(w_query, "ctx", axis=0, tiled=True)).astype(
        jnp.bfloat16
    )
    whole_audio = lax.all_gather(audio_tokens, "ctx", axis=1, tiled=True)
    key_rows = jnp.einsum(
        "sta,ad->std", whole_audio, w_key, preferred_element_type=jnp.float32
    ).astype(jnp.bfloat16)
    value_rows = jnp.einsum(
        "sta,ad->std", whole_audio, w_value, preferred_element_type=jnp.float32
    ).astype(jnp.bfloat16)
    audio_length = key_rows.shape[1]
    position = jnp.arange(rows_dev, dtype=jnp.int32)
    score_scale = 1.0 / HD**0.5
    summed = jnp.zeros((rows_dev, columns), jnp.float32)
    for speaker in range(SPK):
        target = row_lists[speaker]
        row_live = position < row_counts[speaker, 0]
        picked = queries[target].reshape(rows_dev, heads_dev, HD)
        key_block = key_rows[speaker].reshape(audio_length, heads_dev, HD)
        value_block = value_rows[speaker].reshape(audio_length, heads_dev, HD)
        scores = (
            jnp.einsum("rhd,khd->hrk", picked, key_block, preferred_element_type=jnp.float32)
            * score_scale
        )
        scores = scores - jnp.max(scores, axis=-1, keepdims=True)
        weights = jnp.exp(scores)
        weights = (weights / jnp.sum(weights, axis=-1, keepdims=True)).astype(jnp.bfloat16)
        blended = jnp.einsum(
            "hrk,khd->rhd", weights, value_block, preferred_element_type=jnp.float32
        ).astype(jnp.bfloat16)
        blended = blended.reshape(rows_dev, columns).astype(jnp.float32)
        blended = jnp.where(row_live[:, None], blended, jnp.zeros_like(blended))
        summed = summed.at[target].add(blended)
    attended = summed.astype(jnp.bfloat16)
    all_heads = lax.all_gather(attended, "head", axis=1, tiled=True)
    result = add_rows(all_heads, lax.all_gather(w_output, "ctx", axis=0, tiled=True))
    return result.astype(jnp.bfloat16)


def solution(mesh):
    in_specs = (
        P("ctx", None),
        P("ctx", "head"),
        P("ctx", "head"),
        P(None, "ctx", None),
        P(None, "head"),
        P(None, "head"),
        P(None, "ctx"),
        P(None, "ctx"),
    )
    out_specs = P("ctx", "head")
    return jax.shard_map(shards, mesh=mesh, in_specs=in_specs, out_specs=out_specs, check_vma=False)
```

profile of v0, /device:TPU:0, one launch (start us, length us, event | category | flops | bytes accessed | tf_op | source)
XLA Modules:
  0.0 439.1 jit_solution(14626335249302658859)
XLA Ops:
  6.5 0.0 copy-start
  6.5 0.0 copy-start.3
  6.5 0.0 all-gather.4.cloned.1.call-start
  6.5 0.7 all-gather.4.cloned.1.call-update
  7.3 0.0 all-gather.8.cloned.1.call-start
  7.3 0.7 all-gather.8.cloned.1.call-update
  8.0 0.0 all-gather.6.cloned.1.call-start
  8.1 0.0 copy-done.3
  8.1 32.9 %all_gather.12 = bf16[2,32,768]{2,0,1:T(2,128)(2,1)S(1)} all-gather(bf16[2,4,768]{2,0,1:T(2,128)(2,1)S(1)} %copy.25), channel_id=1, replica_groups=mesh['ctx'=8,'head'=4] {'ctx'}, dimensions={1}, use_global_device_ids=true | all-gather | bytes 110592 | tf_op jit(solution)/shard_map/all_gather | solution.py:21
  41.0 0.0 copy-done
  41.0 0.0 copy-start.5
  41.0 0.0 copy-start.4
  41.0 0.5 convolution_convert_fusion.2
  41.5 0.1 reshape_squeeze.13
  41.6 2.0 convolution_convert_fusion.3
  43.6 0.1 reshape_squeeze.12
  43.7 0.1 reshape_squeeze.15
  43.8 0.1 reshape_squeeze.14
  43.8 0.0 copy-done.5
  43.8 0.6 fusion.29
  44.4 0.7 iota_compare_fusion.1
  45.1 0.7 iota_compare_fusion
  45.8 0.0 copy-done.4
  45.8 149.7 %all-gather.4.cloned.1.call-done = bf16[5120,1280]{1,0:T(8,128)(2,1)} async-done(((bf16[640,1280]{1,0:T(8,128)(2,1)}), bf16[5120,1280]{1,0:T(8,128)(2,1)}) %all-gather.4.cloned.1.call-update) | async-done | bytes 13107216 | tf_op jit(solution)/shard_map/all_gather | solution.py:18
  195.5 12.6 %convolution_convert_fusion.1 = bf16[512,1280]{1,0:T(8,128)(2,1)S(1)} fusion(bf16[512,5120]{1,0:T(8,128)(2,1)} %param.8, bf16[5120,1280]{1,0:T(8,128)(2,1)} %all-gather.4.cloned.1.call-done), kind=kOutput, calls=%fused_computation.7 | convolution fusion | flops 6711541760 | bytes 19660800 | tf_op jit(solution)/shard_map/dot_general | solution.py:11
  208.2 2.1 gather_fusion
  210.3 1.5 copy.27
  211.8 1.6 convolution_multiply_fusion.1
  213.4 0.2 fusion.30
  213.6 2.0 fusion.7
  215.6 3.2 copy.32
  218.8 2.1 gather_fusion.1
  221.0 0.7 copy.33
  221.6 0.3 convolution_multiply_fusion
  221.9 0.2 fusion.31
  222.1 2.0 fusion.6
  224.1 0.0 copy-start.2
  224.1 3.4 copy.37
  227.5 0.0 copy-done.2
  227.5 7.2 %scatter_custom_fusion = f32[512,1280]{1,0:T(8,128)} fusion(s32[512]{0:T(512)S(1)} %bitcast.39, f32[]{:T(128)} %constant.5.clone.1, f32[512,1280]{1,0:T(8,128)S(1)} %copy-done.2, pred[512]{0:T(512)(128)(4,1)S(1)} %iota_compare_fusion.1), kind=kCustom, calls=%fused_computation.21 | custom fusion | flops 1310720 | bytes 5244416 | tf_op jit(solution)/shard_map/scatter-add | solution.py:50
  234.7 9.8 %scatter_custom_fusion.1 = f32[512,1280]{1,0:T(8,128)} fusion(f32[512,1280]{1,0:T(8,128)} %scatter_custom_fusion, s32[512]{0:T(512)S(1)} %bitcast.37, f32[512,1280]{1,0:T(8,128)} %copy.37, f32[]{:T(128)} %constant.5.clone.1, pred[512]{0:T(512)(128)(4,1)S(1)} %iota_compare_fusion), kind=kCustom, calls=%fused_computation.8 | custom fusion | flops 1310720 | bytes 5243904 | tf_op jit(solution)/shard_map/scatter-add | solution.py:50
  244.5 2.9 convert_element_type.60
  247.4 0.0 all-gather.6.cloned.1.call-update
  247.4 131.3 %all-gather.8.cloned.1.call-done = bf16[5120,1280]{1,0:T(8,128)(2,1)} async-done(((bf16[640,1280]{1,0:T(8,128)(2,1)}), bf16[5120,1280]{1,0:T(8,128)(2,1)}) %all-gather.8.cloned.1.call-update) | async-done | bytes 13107216 | tf_op jit(solution)/shard_map/all_gather | solution.py:53
  378.8 40.2 %all-gather.6.cloned.1.call-done = bf16[512,5120]{1,0:T(8,128)(2,1)} async-done(((bf16[512,1280]{1,0:T(8,128)(2,1)}), bf16[512,5120]{1,0:T(8,128)(2,1)}) %all-gather.6.cloned.1.call-update) | async-done | bytes 5242896 | tf_op jit(solution)/shard_map/all_gather | solution.py:52
  419.0 0.0 copy-start.1
  419.0 13.6 %convolution_convert_fusion = bf16[512,1280]{1,0:T(8,128)(2,1)} fusion(bf16[512,5120]{1,0:T(8,128)(2,1)} %all-gather.6.cloned.1.call-done, bf16[5120,1280]{1,0:T(8,128)(2,1)} %all-gather.8.cloned.1.call-done), kind=kOutput, calls=%fused_computation.6 | convolution fusion | flops 6711541760 | bytes 19660800 | tf_op jit(solution)/shard_map/dot_general | solution.py:11
  432.6 0.0 copy-done.1
  (6 shorter events, 0.1 us)
Async XLA Ops:
  6.5 34.5 %copy-start = (bf16[768,1280]{1,0:T(8,128)(2,1)S(1)}, bf16[768,1280]{1,0:T(8,128)(2,1)}, u32[]{:S(2)}) copy-start(bf16[768,1280]{1,0:T(8,128)(2,1)} %param.12) | copy-start | bytes 5898244
  6.5 1.5 copy-start.3
  6.5 189.0 %all-gather.4.cloned.1.call-start = ((), (), s32[]{:S(2)}) async-start(), calls=%async_computation | async-start | bytes 14745600 | tf_op jit(solution)/shard_map/all_gather | solution.py:18
  7.3 371.5 %all-gather.8.cloned.1.call-start = ((), (), s32[]{:S(2)}) async-start(), calls=%async_computation.2 | async-start | bytes 14745600 | tf_op jit(solution)/shard_map/all_gather | solution.py:53
  8.0 411.0 %all-gather.6.cloned.1.call-start = ((), (), s32[]{:S(2)}) async-start(), calls=%async_computation.1 | async-start | bytes 6553600 | tf_op jit(solution)/shard_map/all_gather | solution.py:52
  41.0 2.8 copy-start.5
  41.0 4.8 %copy-start.4 = (s32[2,512]{1,0:T(2,128)S(1)}, s32[2,512]{1,0:T(2,128)}, u32[]{:S(2)}) copy-start(s32[2,512]{1,0:T(2,128)} %param.14) | copy-start | bytes 12292
  224.1 3.4 copy-start.2
  419.0 13.6 %copy-start.1 = (bf16[768,1280]{1,0:T(8,128)(2,1)S(1)}, bf16[768,1280]{1,0:T(8,128)(2,1)}, u32[]{:S(2)}) copy-start(bf16[768,1280]{1,0:T(8,128)(2,1)} %param.12) | copy-start | bytes 5898244
Sparse Core Ops, SparseCore 0:
  9.6 185.9 all-gather.3
  197.7 180.9 all-gather.7
  380.3 38.6 all-gather.5
where the time goes:
time: 439 us
  waiting for transfers between devices  323 us (74%)
  matrix products  34.7 us (8%)
  blocking collectives  32.9 us (7%)
  other arithmetic  21.6 us (5%)
  local copies, waits for them, and re-layouts  13.9 us (3%)
  between operations  13.3 us (3%)
    all_gather x1, waiting for transfers between devices, shards(): lax.all_gather(w_query, 'ctx', axis=0, tiled=True)  150 us
    all_gather x1, waiting for transfers between devices, shards(): lax.all_gather(w_output, 'ctx', axis=0, tiled=True)  131 us
    all_gather x1, waiting for transfers between devices, shards(): all_heads = lax.all_gather(attended, 'head', axis=1, tiled=True)  40.2 us
    all_gather x1, blocking collectives, shards(): whole_audio = lax.all_gather(audio_tokens, 'ctx', axis=1, tiled=True)  32.9 us
    dot_general x2, matrix products, add_rows(): return jnp.dot(left_rows, shard_piece, preferred_element_type=jnp.float32)  26.2 us
    scatter-add x2, other arithmetic, shards(): summed = summed.at[target].add(blended)  17 us
  transfers between devices with their start and end apart: 3, of which 3 were waited for; matrix products, arithmetic and copies ran while one was open for 13% of the time, Pallas kernels for 0%

commit v1 on v0

--- a/solution.py
+++ b/solution.py
@@ -18,7 +18,12 @@
     queries = add_rows(video_rows, lax.all_gather(w_query, "ctx", axis=0, tiled=True)).astype(
         jnp.bfloat16
     )
-    whole_audio = lax.all_gather(audio_tokens, "ctx", axis=1, tiled=True)
+    ring = [audio_tokens]
+    for hop in range(7):
+        ring.append(lax.ppermute(ring[-1], "ctx", [(dev, (dev + 1) % 8) for dev in range(8)]))
+    whole_audio = jnp.roll(
+        jnp.concatenate(ring[::-1], axis=1), (lax.axis_index("ctx") + 1) * ring[0].shape[1], axis=1
+    )
     key_rows = jnp.einsum(
         "sta,ad->std", whole_audio, w_key, preferred_element_type=jnp.float32
     ).astype(jnp.bfloat16)

time: 439 us -> 440 us (level)
  waiting for transfers between devices: 323 us -> 356 us
  blocking collectives: 32.9 us -> 0 us
    ppermute x0 -> x7, waiting for transfers between devices: none -> 42.7 us  [shards(): lax.ppermute(ring[-1], 'ctx', [(dev, (dev + 1) % 8) for dev in range(8)])]
    all_gather x1 -> x0, blocking collectives: 32.9 us -> none  [shards(): whole_audio = lax.all_gather(audio_tokens, 'ctx', axis=1, tiled=True)]
    all_gather x1, waiting for transfers between devices: 150 us -> 138 us  [shards(): lax.all_gather(w_query, 'ctx', axis=0, tiled=True)]
  transfers between devices with their start and end apart: 3 -> 10, of which waited for: 3 -> 10; matrix products, arithmetic and copies ran while one was open for 13% -> 12% of each run, Pallas kernels for 0% -> 0%
where the time goes in v1:
time: 440 us
  waiting for transfers between devices  356 us (81%)
  matrix products  33.2 us (8%)
  other arithmetic  21.8 us (5%)
  between operations  13.3 us (3%)
  local copies, waits for them, and re-layouts  12.8 us (3%)
    all_gather x1, waiting for transfers between devices, shards(): lax.all_gather(w_query, 'ctx', axis=0, tiled=True)  138 us
    all_gather x1, waiting for transfers between devices, shards(): lax.all_gather(w_output, 'ctx', axis=0, tiled=True)  134 us
    ppermute x7, waiting for transfers between devices, shards(): lax.ppermute(ring[-1], 'ctx', [(dev, (dev + 1) % 8) for dev in range(8)])  42.7 us
    all_gather x1, waiting for transfers between devices, shards(): all_heads = lax.all_gather(attended, 'head', axis=1, tiled=True)  40.2 us
    dot_general x2, matrix products, add_rows(): return jnp.dot(left_rows, shard_piece, preferred_element_type=jnp.float32)  26.2 us
    scatter-add x2, other arithmetic, shards(): summed = summed.at[target].add(blended)  17.2 us
  transfers between devices with their start and end apart: 10, of which 10 were waited for; matrix products, arithmetic and copies ran while one was open for 12% of the time, Pallas kernels for 0%

profile of v1, /device:TPU:0, one launch (start us, length us, event | category | flops | bytes accessed | tf_op | source)
XLA Modules:
  0.0 439.8 jit_solution(13393725382631965448)
XLA Ops:
  6.5 0.0 all-gather.4.cloned.1.call-start
  6.6 0.7 all-gather.4.cloned.1.call-update
  7.3 0.0 all-gather.8.cloned.1.call-start
  7.3 0.7 all-gather.8.cloned.1.call-update
  8.0 0.0 all-gather.6.cloned.1.call-start
  8.1 3.0 collective-permute-start
  11.1 4.7 %collective-permute-done = bf16[2,4,768]{2,1,0:T(4,128)(2,1)S(1)} collective-permute-done((bf16[2,4,768]{2,1,0:T(4,128)(2,1)S(1)}, bf16[2,4,768]{2,1,0:T(4,128)(2,1)S(1)}, u32[]{:S(2)}, u32[]{:S(2)}) %collective-permute-start) | collective-permute-done | bytes 12320 | tf_op jit(solution)/shard_map/ppermute | solution.py:23
  15.8 0.0 collective-permute-start.1
  15.8 6.4 %collective-permute-done.1 = bf16[2,4,768]{2,1,0:T(4,128)(2,1)S(1)} collective-permute-done((bf16[2,4,768]{2,1,0:T(4,128)(2,1)S(1)}, bf16[2,4,768]{2,1,0:T(4,128)(2,1)S(1)}, u32[]{:S(2)}, u32[]{:S(2)}) %collective-permute-start.1) | collective-permute-done | bytes 12320 | tf_op jit(solution)/shard_map/ppermute | solution.py:23
  22.2 0.0 collective-permute-start.2
  22.2 0.6 fusion.31
  22.8 6.0 %collective-permute-done.2 = bf16[2,4,768]{2,1,0:T(4,128)(2,1)S(1)} collective-permute-done((bf16[2,4,768]{2,1,0:T(4,128)(2,1)S(1)}, bf16[2,4,768]{2,1,0:T(4,128)(2,1)S(1)}, u32[]{:S(2)}, u32[]{:S(2)}) %collective-permute-start.2) | collective-permute-done | bytes 12320 | tf_op jit(solution)/shard_map/ppermute | solution.py:23
  28.8 6.7 %collective-permute-done.3 = bf16[2,4,768]{2,1,0:T(4,128)(2,1)S(1)} collective-permute-done((bf16[2,4,768]{2,1,0:T(4,128)(2,1)S(1)}, bf16[2,4,768]{2,1,0:T(4,128)(2,1)S(1)}, u32[]{:S(2)}, u32[]{:S(2)}) %collective-permute-start.3) | collective-permute-done | bytes 12320 | tf_op jit(solution)/shard_map/ppermute | solution.py:23
  35.5 0.0 collective-permute-start.4
  35.5 6.8 %collective-permute-done.4 = bf16[2,4,768]{2,1,0:T(4,128)(2,1)S(1)} collective-permute-done((bf16[2,4,768]{2,1,0:T(4,128)(2,1)S(1)}, bf16[2,4,768]{2,1,0:T(4,128)(2,1)S(1)}, u32[]{:S(2)}, u32[]{:S(2)}) %collective-permute-start.4) | collective-permute-done | bytes 12320 | tf_op jit(solution)/shard_map/ppermute | solution.py:23
  42.3 0.0 collective-permute-start.5
  42.3 0.6 iota_compare_fusion.1
  43.0 6.0 %collective-permute-done.5 = bf16[2,4,768]{2,1,0:T(4,128)(2,1)S(1)} collective-permute-done((bf16[2,4,768]{2,1,0:T(4,128)(2,1)S(1)}, bf16[2,4,768]{2,1,0:T(4,128)(2,1)S(1)}, u32[]{:S(2)}, u32[]{:S(2)}) %collective-permute-start.5) | collective-permute-done | bytes 12320 | tf_op jit(solution)/shard_map/ppermute | solution.py:23
  49.0 0.7 iota_compare_fusion
  49.7 6.0 %collective-permute-done.6 = bf16[2,4,768]{2,1,0:T(4,128)(2,1)S(1)} collective-permute-done((bf16[2,4,768]{2,1,0:T(4,128)(2,1)S(1)}, bf16[2,4,768]{2,1,0:T(4,128)(2,1)S(1)}, u32[]{:S(2)}, u32[]{:S(2)}) %collective-permute-start.6) | collective-permute-done | bytes 12320 | tf_op jit(solution)/shard_map/ppermute | solution.py:23
  55.7 0.2 concatenate.6
  56.0 0.5 convolution_convert_fusion.2
  56.4 0.1 reshape_squeeze.15
  56.5 2.0 convolution_convert_fusion.3
  58.5 0.1 reshape_squeeze.14
  58.6 0.1 reshape_squeeze.13
  58.7 0.1 reshape_squeeze.12
  58.7 137.5 %all-gather.4.cloned.1.call-done = bf16[5120,1280]{1,0:T(8,128)(2,1)} async-done(((bf16[640,1280]{1,0:T(8,128)(2,1)}), bf16[5120,1280]{1,0:T(8,128)(2,1)}) %all-gather.4.cloned.1.call-update) | async-done | bytes 13107216 | tf_op jit(solution)/shard_map/all_gather | solution.py:18
  196.3 12.6 %convolution_convert_fusion.1 = bf16[512,1280]{1,0:T(8,128)(2,1)S(1)} fusion(bf16[512,5120]{1,0:T(8,128)(2,1)} %param.8, bf16[5120,1280]{1,0:T(8,128)(2,1)} %all-gather.4.cloned.1.call-done), kind=kOutput, calls=%fused_computation.7 | convolution fusion | flops 6711541760 | bytes 19660800 | tf_op jit(solution)/shard_map/dot_general | solution.py:11
  208.9 2.1 gather_fusion.1
  211.0 1.5 copy.20
  212.5 1.6 convolution_multiply_fusion
  214.1 0.2 fusion.33
  214.3 2.1 fusion.6
  216.4 3.2 copy.24
  219.6 2.1 gather_fusion
  221.7 0.7 copy.15
  222.4 0.3 convolution_multiply_fusion.1
  222.7 0.2 fusion.32
  222.9 0.6 fusion.7
  223.5 2.1 copy.19
  225.6 8.6 %scatter_custom_fusion = f32[512,1280]{1,0:T(8,128)} fusion(s32[512]{0:T(512)S(1)} %bitcast.39, f32[]{:T(128)} %constant.30.clone.1, f32[512,1280]{1,0:T(8,128)} %copy.19, pred[512]{0:T(512)(128)(4,1)S(1)} %iota_compare_fusion.1), kind=kCustom, calls=%fused_computation.21 | custom fusion | flops 1310720 | bytes 5244416 | tf_op jit(solution)/shard_map/scatter-add | solution.py:55
  234.1 8.6 %scatter_custom_fusion.1 = f32[512,1280]{1,0:T(8,128)} fusion(f32[512,1280]{1,0:T(8,128)} %scatter_custom_fusion, s32[512]{0:T(512)S(1)} %bitcast.37, f32[512,1280]{1,0:T(8,128)S(1)} %copy-done.2, f32[]{:T(128)} %constant.30.clone.1, pred[512]{0:T(512)(128)(4,1)S(1)} %iota_compare_fusion), kind=kCustom, calls=%fused_computation.8 | custom fusion | flops 1310720 | bytes 5243904 | tf_op jit(solution)/shard_map/scatter-add | solution.py:55
  242.8 3.0 convert_element_type.60
  245.7 0.0 all-gather.6.cloned.1.call-update
  245.7 133.7 %all-gather.8.cloned.1.call-done = bf16[5120,1280]{1,0:T(8,128)(2,1)} async-done(((bf16[640,1280]{1,0:T(8,128)(2,1)}), bf16[5120,1280]{1,0:T(8,128)(2,1)}) %all-gather.8.cloned.1.call-update) | async-done | bytes 13107216 | tf_op jit(solution)/shard_map/all_gather | solution.py:58
  379.5 40.2 %all-gather.6.cloned.1.call-done = bf16[512,5120]{1,0:T(8,128)(2,1)} async-done(((bf16[512,1280]{1,0:T(8,128)(2,1)}), bf16[512,5120]{1,0:T(8,128)(2,1)}) %all-gather.6.cloned.1.call-update) | async-done | bytes 5242896 | tf_op jit(solution)/shard_map/all_gather | solution.py:57
  419.7 13.6 %convolution_convert_fusion = bf16[512,1280]{1,0:T(8,128)(2,1)} fusion(bf16[512,5120]{1,0:T(8,128)(2,1)} %all-gather.6.cloned.1.call-done, bf16[5120,1280]{1,0:T(8,128)(2,1)} %all-gather.8.cloned.1.call-done), kind=kOutput, calls=%fused_computation.6 | convolution fusion | flops 6711541760 | bytes 19660800 | tf_op jit(solution)/shard_map/dot_general | solution.py:11
  (19 shorter events, 0.1 us)
Async XLA Ops:
  6.5 49.4 %copy-start = (bf16[768,1280]{1,0:T(8,128)(2,1)S(1)}, bf16[768,1280]{1,0:T(8,128)(2,1)}, u32[]{:S(2)}) copy-start(bf16[768,1280]{1,0:T(8,128)(2,1)} %param.12) | copy-start | bytes 5898244
  6.5 1.5 copy-start.3
  6.5 9.2 %copy-start.4 = (s32[2,512]{1,0:T(2,128)S(1)}, s32[2,512]{1,0:T(2,128)}, u32[]{:S(2)}) copy-start(s32[2,512]{1,0:T(2,128)} %param.14) | copy-start | bytes 12292
  6.5 15.6 %copy-start.5 = (s32[2,1]{0,1:T(1,128)S(1)}, s32[2,1]{0,1:T(1,128)}, u32[]{:S(2)}) copy-start(s32[2,1]{0,1:T(1,128)} %param.15) | copy-start | bytes 28
  6.5 189.7 %all-gather.4.cloned.1.call-start = ((), (), s32[]{:S(2)}) async-start(), calls=%async_computation | async-start | bytes 14745600 | tf_op jit(solution)/shard_map/all_gather | solution.py:18
  7.3 372.2 %all-gather.8.cloned.1.call-start = ((), (), s32[]{:S(2)}) async-start(), calls=%async_computation.2 | async-start | bytes 14745600 | tf_op jit(solution)/shard_map/all_gather | solution.py:58
  8.0 411.7 %all-gather.6.cloned.1.call-start = ((), (), s32[]{:S(2)}) async-start(), calls=%async_computation.1 | async-start | bytes 6553600 | tf_op jit(solution)/shard_map/all_gather | solution.py:57
  8.1 7.7 %collective-permute-start = (bf16[2,4,768]{2,1,0:T(4,128)(2,1)S(1)}, bf16[2,4,768]{2,1,0:T(4,128)(2,1)S(1)}, u32[]{:S(2)}, u32[]{:S(2)}) collective-permute-start(bf16[2,4,768]{2,1,0:T(4,128)(2,1)S(1)} %copy-done.3), channel_id=1, source_target_pairs={{0,4},{4,8},{8,12},{12,16},{16,20},{20,24},{24,28},{28,0},{1,5},{5... | collective-permute-start | bytes 36872 | tf_op jit(solution)/shard_map/ppermute | solution.py:23
  15.8 6.4 %collective-permute-start.1 = (bf16[2,4,768]{2,1,0:T(4,128)(2,1)S(1)}, bf16[2,4,768]{2,1,0:T(4,128)(2,1)S(1)}, u32[]{:S(2)}, u32[]{:S(2)}) collective-permute-start(bf16[2,4,768]{2,1,0:T(4,128)(2,1)S(1)} %collective-permute-done), channel_id=1, source_target_pairs={{0,4},{4,8},{8,12},{12,16},{16,20},{20,24},{24,28},{28,0},{1,5},{5... | collective-permute-start | bytes 36872 | tf_op jit(solution)/shard_map/ppermute | solution.py:23
  22.2 6.6 %collective-permute-start.2 = (bf16[2,4,768]{2,1,0:T(4,128)(2,1)S(1)}, bf16[2,4,768]{2,1,0:T(4,128)(2,1)S(1)}, u32[]{:S(2)}, u32[]{:S(2)}) collective-permute-start(bf16[2,4,768]{2,1,0:T(4,128)(2,1)S(1)} %collective-permute-done.1), channel_id=1, source_target_pairs={{0,4},{4,8},{8,12},{12,16},{16,20},{20,24},{24,28},{28,0},{1,5},{5... | collective-permute-start | bytes 36872 | tf_op jit(solution)/shard_map/ppermute | solution.py:23
  28.7 6.7 %collective-permute-start.3 = (bf16[2,4,768]{2,1,0:T(4,128)(2,1)S(1)}, bf16[2,4,768]{2,1,0:T(4,128)(2,1)S(1)}, u32[]{:S(2)}, u32[]{:S(2)}) collective-permute-start(bf16[2,4,768]{2,1,0:T(4,128)(2,1)S(1)} %collective-permute-done.2), channel_id=1, source_target_pairs={{0,4},{4,8},{8,12},{12,16},{16,20},{20,24},{24,28},{28,0},{1,5},{5... | collective-permute-start | bytes 36872 | tf_op jit(solution)/shard_map/ppermute | solution.py:23
  35.5 6.8 %collective-permute-start.4 = (bf16[2,4,768]{2,1,0:T(4,128)(2,1)S(1)}, bf16[2,4,768]{2,1,0:T(4,128)(2,1)S(1)}, u32[]{:S(2)}, u32[]{:S(2)}) collective-permute-start(bf16[2,4,768]{2,1,0:T(4,128)(2,1)S(1)} %collective-permute-done.3), channel_id=1, source_target_pairs={{0,4},{4,8},{8,12},{12,16},{16,20},{20,24},{24,28},{28,0},{1,5},{5... | collective-permute-start | bytes 36872 | tf_op jit(solution)/shard_map/ppermute | solution.py:23
  42.3 6.7 %collective-permute-start.5 = (bf16[2,4,768]{2,1,0:T(4,128)(2,1)S(1)}, bf16[2,4,768]{2,1,0:T(4,128)(2,1)S(1)}, u32[]{:S(2)}, u32[]{:S(2)}) collective-permute-start(bf16[2,4,768]{2,1,0:T(4,128)(2,1)S(1)} %collective-permute-done.4), channel_id=1, source_target_pairs={{0,4},{4,8},{8,12},{12,16},{16,20},{20,24},{24,28},{28,0},{1,5},{5... | collective-permute-start | bytes 36872 | tf_op jit(solution)/shard_map/ppermute | solution.py:23
  49.0 6.7 %collective-permute-start.6 = (bf16[2,4,768]{2,1,0:T(4,128)(2,1)S(1)}, bf16[2,4,768]{2,1,0:T(4,128)(2,1)S(1)}, u32[]{:S(2)}, u32[]{:S(2)}) collective-permute-start(bf16[2,4,768]{2,1,0:T(4,128)(2,1)S(1)} %collective-permute-done.5), channel_id=1, source_target_pairs={{0,4},{4,8},{8,12},{12,16},{16,20},{20,24},{24,28},{28,0},{1,5},{5... | collective-permute-start | bytes 36872 | tf_op jit(solution)/shard_map/ppermute | solution.py:23
  225.6 8.6 %copy-start.2 = (f32[512,1280]{1,0:T(8,128)S(1)}, f32[512,1280]{1,0:T(8,128)}, u32[]{:S(2)}) copy-start(f32[512,1280]{1,0:T(8,128)} %copy.24) | copy-start | bytes 7864324
  419.7 13.6 %copy-start.1 = (bf16[768,1280]{1,0:T(8,128)(2,1)S(1)}, bf16[768,1280]{1,0:T(8,128)(2,1)}, u32[]{:S(2)}) copy-start(bf16[768,1280]{1,0:T(8,128)(2,1)} %param.12) | copy-start | bytes 5898244
Sparse Core Ops, SparseCore 0:
  9.6 186.6 all-gather.3
  198.4 180.9 all-gather.7
  381.1 38.6 all-gather.5
